TPU v7x, 32 devices: a whole 2x2x4 slice. The times are simulated.
32 devices in a mesh: chi: 4 (over y, x), dl: 4 (over z), cell: 2 (over core).
Axes of the slice: x: 2, y: 2, z: 4, core: 2. Of those that a mesh axis runs over, the one named last changes fastest.
Arguments:
- left_env: bfloat16 [2, 512, 512, 36], P('cell', None, 'chi'), may hold values from -6 to 6
- up_left: bfloat16 [2, 512, 36, 512], P('cell', 'chi', None, 'dl'), may hold values from -0.109375 to 0.109375
- up_center: bfloat16 [2, 512, 36, 512], P('cell', 'chi', None, 'dl'), may hold values from -0.109375 to 0.109375
- right_env: bfloat16 [2, 512, 36, 512], P('cell', 'dl'), may hold values from -0.046875 to 0.046875
- center: bfloat16 [2, 512, 512], P('cell', None, 'dl'), may hold values from -0.25 to 0.25
- ket_tensor: bfloat16 [2, 6, 6, 6, 6, 2], P('cell'), may hold values from -0.875 to 0.875
Outputs:
- left_env_new: float32 [2, 512, 36, 512], P('cell', 'chi', None, 'dl')
- new_left: float32 [2, 512, 36, 512], P('cell', 'chi', None, 'dl')
All inputs are finite; a program needn't handle non-finite values.
Results may differ from a plain program's by a relative error of at most 0.0066.
The roundings to bfloat16 on the way count: a program that leaves them out, or rounds other values in their place, can miss the bound.
Values may be sent and summed in bfloat16 or wider, within the bound.
A program may use at most 256 MiB of HBM per device.

v0:
```python
from functools import partial
import math
import jax
import jax.numpy as jnp
from jax import lax
from jax.sharding import PartitionSpec as P

ITERS = 5
HIGHEST = lax.Precision.HIGHEST


def from_behind(block, axis, distance):
    devices = range(lax.axis_size(axis))
    route = [((i - distance) % len(devices), i) for i in devices]
    return lax.ppermute(block, axis, route)


def layered(block, tensor):
    leg_size = tensor.shape[0]
    amount = block.shape[0]
    columns = block.shape[3]
    unfolded = block.reshape(amount, leg_size, leg_size, leg_size, leg_size, columns)
    ket_side = jnp.einsum(
        "blLuUc,lurdp->bLUcrdp", unfolded, tensor, preferred_element_type=jnp.float32
    ).astype(jnp.bfloat16)
    both_sides = jnp.einsum(
        "bLUcrdp,LUsep->brsdec", ket_side, tensor, preferred_element_type=jnp.float32
    )
    return both_sides.reshape(amount, leg_size * leg_size, leg_size * leg_size, columns).astype(
        jnp.bfloat16
    )


def through_site(stacked, tensor):
    amount = stacked.shape[0]
    stride = min(amount, 8)
    blocks = stacked.reshape((amount // stride, stride) + stacked.shape[1:])
    finished = lax.map(partial(layered, tensor=tensor), blocks)
    return finished.reshape((amount,) + finished.shape[2:])


def shards(left_env, up_left, up_center, right_env, center, ket_tensor):
    env_local = left_env[0]
    left_iso = up_left[0]
    left_mid = up_center[0]
    env_right = right_env[0]
    bond_mat = center[0]
    site_ket = ket_tensor[0]
    chi_all = env_local.shape[0]
    leg_width = env_local.shape[2]
    col_count = left_iso.shape[2]
    iso_all, mid_all = (
        lax.all_gather(left_iso, "chi", axis=0, tiled=True),
        lax.all_gather(left_mid, "chi", axis=0, tiled=True),
    )
    left_sum = jnp.einsum("abm,asc->bmsc", env_local, iso_all, preferred_element_type=jnp.float32)
    left_cut = through_site(left_sum.astype(jnp.bfloat16), site_ket)
    right_sum = jnp.einsum("abm,asc->bmsc", env_local, mid_all, preferred_element_type=jnp.float32)
    right_cut = through_site(right_sum.astype(jnp.bfloat16), site_ket)
    next_iso = from_behind(left_iso, "cell", -1)
    bra_iso = lax.all_gather(next_iso, "dl", axis=2, tiled=True)
    env_new = lax.psum_scatter(
        jnp.einsum("bmdc,bdk->kmc", left_cut, bra_iso, preferred_element_type=jnp.float32),
        "chi",
        scatter_dimension=0,
        tiled=True,
    )
    center_term = jnp.einsum(
        "bmda,amc->cbd", right_cut, env_right, preferred_element_type=jnp.float32
    )
    mixed = jnp.einsum(
        "abm,ax->bmx", env_local, bond_mat, preferred_element_type=jnp.float32
    ).astype(jnp.bfloat16)
    bond_term = jnp.einsum("bma,amc->cb", mixed, env_right, preferred_element_type=jnp.float32)
    center_part, bond_part = (
        lax.psum_scatter(center_term, "dl", scatter_dimension=0, tiled=True),
        lax.psum_scatter(bond_term, "dl", scatter_dimension=0, tiled=True),
    )
    center_all, bond_cols = (
        lax.all_gather(center_part.astype(jnp.bfloat16), "dl", axis=0, tiled=True),
        lax.all_gather(bond_part.astype(jnp.bfloat16), "dl", axis=0, tiled=True),
    )
    bond_full = lax.all_gather(bond_cols, "chi", axis=1, tiled=True)
    bond_mine = lax.dynamic_slice_in_dim(bond_full, lax.axis_index("dl") * col_count, col_count, 1)
    target = jnp.einsum("cbd,cx->bdx", center_all, bond_mine, preferred_element_type=jnp.float32)
    factor = 0.25 * math.sqrt(chi_all)
    norm_sum = lax.psum(jnp.sum(target * target), ("chi", "dl"))
    current = target * (factor / jnp.sqrt(norm_sum))
    for sweep_index in range(ITERS):
        spread = lax.all_gather(current.astype(jnp.bfloat16), "dl", axis=2, tiled=True).astype(
            current.dtype
        )
        gram_rows = lax.psum(
            jnp.einsum("bdx,bdy->xy", current, spread, precision=HIGHEST).astype(jnp.bfloat16),
            "chi",
        ).astype(jnp.float32)
        current = 1.5 * current - 0.5 * jnp.einsum(
            "bdy,xy->bdx", spread, gram_rows, precision=HIGHEST
        )
    new_left = current * math.sqrt(chi_all * leg_width)
    return (env_new[None], new_left[None])


def solution(mesh):
    placed = (
        P("cell", None, "chi", None),
        P("cell", "chi", None, "dl"),
        P("cell", "chi", None, "dl"),
        P("cell", "dl", None, None),
        P("cell", None, "dl"),
        P("cell", None, None, None, None, None),
    )
    return jax.shard_map(
        shards,
        mesh=mesh,
        in_specs=placed,
        out_specs=(P("cell", "chi", None, "dl"), P("cell", "chi", None, "dl")),
        check_vma=False,
    )
```

profile of v0, /device:TPU:0, one launch (start us, length us, event | category | flops | bytes accessed | tf_op | source)
XLA Modules:
  0.0 1720.3 jit_solution(1469185994787700763)
XLA Ops:
  9.4 60.3 %all-gather.28.cloned.1.call-done = bf16[1,512,36,128]{3,1,2,0:T(8,128)(2,1)} async-done(((bf16[1,128,36,128]{3,1,2,0:T(8,128)(2,1)}), bf16[1,512,36,128]{3,1,2,0:T(8,128)(2,1)}) %all-gather.28.cloned.1.call-update) | async-done | bytes 4718608 | tf_op jit(solution)/shard_map/all_gather | solution.py:54
  69.7 29.6 %convert_bitcast_fusion = bf16[16,8,36,36,128]{4,1,0,3,2:T(8,128)(2,1)} fusion(bf16[1,512,128,36]{2,1,3,0:T(8,128)(2,1)} %param.10, bf16[1,512,36,128]{3,1,2,0:T(8,128)(2,1)} %all-gather.28.cloned.1.call-done), kind=kOutput, calls=%fused_computation.26 | convolution fusion | flops 21764505600 | bytes 51904512 | tf_op jit(solution)/shard_map/abm,asc->bmsc/dot_general | solution.py:58
  99.2 14.1 broadcast.9.clone2.1
  113.3 220.6 %while.21 = (s32[]{:T(128)}, bf16[16,8,36,36,128]{4,1,0,3,2:T(8,128)(2,1)}, bf16[16,8,36,36,128]{4,1,0,3,2:T(8,128)(2,1)}, bf16[6,6,6,6,2]{1,3,4,0,2:T(8,128)(2,1)S(1)}, s32[]{:T(128)}) while((s32[]{:T(128)}, bf16[16,8,36,36,128]{4,1,0,3,2:T(8,128)(2,1)}, bf16[16,8,36,36,128]{4,1,0,3,2:T(8,128)(2,1)}, bf16[6,6,6,6,2]{1,3,4,0,2:T(8,128)(2,1)S(1)}, ...), condition=%wide.region_4.5_spmd, body=%wide.region_3.4_spmd.sunk | while | flops 386187264 | bytes 31861440 | solution.py:38
  117.9 4.3 fusion.122
  131.7 4.3 fusion.122
  145.6 4.3 fusion.122
  159.4 4.3 fusion.122
  173.2 4.3 fusion.122
  186.9 4.3 fusion.122
  200.7 4.3 fusion.122
  214.5 4.3 fusion.122
  228.3 4.3 fusion.122
  242.1 4.3 fusion.122
  255.9 4.3 fusion.122
  269.7 4.3 fusion.122
  283.5 4.3 fusion.122
  297.3 4.3 fusion.122
  311.0 4.3 fusion.122
  324.8 4.3 fusion.122
  334.0 28.7 %fusion.37 = f32[512,128,36]{0,1,2:T(8,128)} fusion(bf16[1,128,36,512]{3,1,2,0:T(8,128)(2,1)} %param.13, bf16[16,8,36,36,128]{4,1,0,3,2:T(8,128)(2,1)} %get-tuple-element.47), kind=kOutput, calls=%fused_computation.39 | convolution fusion | flops 21743271936 | bytes 56623104 | tf_op jit(solution)/shard_map/bmda,amc->cbd/dot_general | solution.py:68
  362.7 7.2 fusion.51
  370.0 154.1 %reduce-scatter.6.cloned.1.call-done = f32[128,128,36]{0,1,2:T(8,128)} async-done(((f32[512,128,36]{0,1,2:T(8,128)}), f32[128,128,36]{0,1,2:T(8,128)}) %reduce-scatter.6.cloned.1.call-update) | async-done | bytes 2359312 | tf_op jit(solution)/shard_map/reduce_scatter | solution.py:76
  527.0 20.4 %reduce-scatter.8.cloned.1.call-done = f32[128,128]{0,1:T(8,128)} async-done(((f32[512,128]{0,1:T(8,128)}), f32[128,128]{0,1:T(8,128)}) %reduce-scatter.8.cloned.1.call-update) | async-done | bytes 65552 | tf_op jit(solution)/shard_map/reduce_scatter | solution.py:77
  548.3 12.3 all_gather.37
  560.6 10.0 all_gather.38
  570.6 68.2 %all-gather.14.cloned.1.call-done = bf16[512,128,36]{0,1,2:T(8,128)(2,1)} async-done(((bf16[128,128,36]{0,1,2:T(8,128)(2,1)}), bf16[512,128,36]{0,1,2:T(8,128)(2,1)}) %all-gather.14.cloned.1.call-update) | async-done | bytes 4718608 | tf_op jit(solution)/shard_map/all_gather | solution.py:80
  638.8 4.3 multiply_reduce_fusion
  643.1 38.9 %psum.42 = f32[]{:T(128)} all-reduce(f32[]{:T(128)} %get-tuple-element.94), channel_id=1, replica_groups=mesh['chi'=4,'dl'=4,'cell'=2] {'chi','dl'}, use_global_device_ids=true, to_apply=%region_8.9 | all-reduce | flops 1 | bytes 8 | tf_op jit(solution)/shard_map/psum | solution.py:87
  684.1 86.6 %all-gather.16.cloned.1.call-done = bf16[128,36,512]{2,0,1:T(8,128)(2,1)} async-done(((bf16[128,36,128]{2,0,1:T(8,128)(2,1)}), bf16[128,36,512]{2,0,1:T(8,128)(2,1)}) %all-gather.16.cloned.1.call-update) | async-done | bytes 4718608 | tf_op jit(solution)/shard_map/all_gather | solution.py:90
  770.7 5.5 fusion.58
  776.2 40.3 %all-reduce.6.cloned.1.call-done = bf16[128,512]{1,0:T(8,128)(2,1)} async-done(((bf16[128,512]{1,0:T(8,128)(2,1)}), bf16[128,512]{1,0:T(8,128)(2,1)}) %all-reduce.6.cloned.1.call-update) | async-done | bytes 131088 | tf_op jit(solution)/shard_map/psum | solution.py:93
  816.5 5.5 fusion.74
  822.3 89.0 %all-gather.18.cloned.1.call-done = bf16[128,36,512]{2,0,1:T(8,128)(2,1)} async-done(((bf16[128,36,128]{2,0,1:T(8,128)(2,1)}), bf16[128,36,512]{2,0,1:T(8,128)(2,1)}) %all-gather.18.cloned.1.call-update) | async-done | bytes 4718608 | tf_op jit(solution)/shard_map/all_gather | solution.py:90
  911.4 6.2 fusion.54
  917.6 40.3 %all-reduce.8.cloned.1.call-done = bf16[128,512]{1,0:T(8,128)(2,1)} async-done(((bf16[128,512]{1,0:T(8,128)(2,1)}), bf16[128,512]{1,0:T(8,128)(2,1)}) %all-reduce.8.cloned.1.call-update) | async-done | bytes 131088 | tf_op jit(solution)/shard_map/psum | solution.py:93
  957.9 5.5 fusion.75
  963.5 89.2 %all-gather.20.cloned.1.call-done = bf16[128,36,512]{2,0,1:T(8,128)(2,1)} async-done(((bf16[128,36,128]{2,0,1:T(8,128)(2,1)}), bf16[128,36,512]{2,0,1:T(8,128)(2,1)}) %all-gather.20.cloned.1.call-update) | async-done | bytes 4718608 | tf_op jit(solution)/shard_map/all_gather | solution.py:90
  1052.7 6.2 fusion.55
  1059.0 40.3 %all-reduce.10.cloned.1.call-done = bf16[128,512]{1,0:T(8,128)(2,1)} async-done(((bf16[128,512]{1,0:T(8,128)(2,1)}), bf16[128,512]{1,0:T(8,128)(2,1)}) %all-reduce.10.cloned.1.call-update) | async-done | bytes 131088 | tf_op jit(solution)/shard_map/psum | solution.py:93
  1099.3 5.6 fusion.76
  1105.6 88.6 %all-gather.22.cloned.1.call-done = bf16[128,36,512]{2,0,1:T(8,128)(2,1)} async-done(((bf16[128,36,128]{2,0,1:T(8,128)(2,1)}), bf16[128,36,512]{2,0,1:T(8,128)(2,1)}) %all-gather.22.cloned.1.call-update) | async-done | bytes 4718608 | tf_op jit(solution)/shard_map/all_gather | solution.py:90
  1194.1 5.5 fusion.56
  1200.7 50.5 %all-gather.26.cloned.1.call-done = bf16[1,512,36,128]{3,1,2,0:T(8,128)(2,1)} async-done(((bf16[1,128,36,128]{3,1,2,0:T(8,128)(2,1)}), bf16[1,512,36,128]{3,1,2,0:T(8,128)(2,1)}) %all-gather.26.cloned.1.call-update) | async-done | bytes 4718608 | tf_op jit(solution)/shard_map/all_gather | solution.py:53
  1251.1 29.6 %convert_bitcast_fusion.1 = bf16[16,8,36,36,128]{4,1,0,3,2:T(8,128)(2,1)} fusion(bf16[1,512,128,36]{2,1,3,0:T(8,128)(2,1)} %param.10, bf16[1,512,36,128]{3,1,2,0:T(8,128)(2,1)} %all-gather.26.cloned.1.call-done), kind=kOutput, calls=%fused_computation.27 | convolution fusion | flops 21764505600 | bytes 51904512 | tf_op jit(solution)/shard_map/abm,asc->bmsc/dot_general | solution.py:56
  1280.7 15.9 all-reduce.12.cloned.1.call-done
  1296.6 5.5 fusion.77
  1302.4 14.7 broadcast.9.clone2
  1317.1 220.8 %while.20 = (s32[]{:T(128)}, bf16[16,8,36,36,128]{4,1,0,3,2:T(8,128)(2,1)}, bf16[16,8,36,36,128]{4,1,0,3,2:T(8,128)(2,1)}, bf16[6,6,6,6,2]{1,3,4,0,2:T(8,128)(2,1)S(1)}, s32[]{:T(128)}) while((s32[]{:T(128)}, bf16[16,8,36,36,128]{4,1,0,3,2:T(8,128)(2,1)}, bf16[16,8,36,36,128]{4,1,0,3,2:T(8,128)(2,1)}, bf16[6,6,6,6,2]{1,3,4,0,2:T(8,128)(2,1)S(1)}, ...), condition=%wide.region_1.2_spmd, body=%wide.region_0.1_spmd.sunk | while | flops 386187264 | bytes 31861440 | solution.py:38
  1321.7 4.3 fusion.115
  1335.5 4.3 fusion.115
  1349.3 4.3 fusion.115
  1363.2 4.3 fusion.115
  1376.9 4.3 fusion.115
  1404.5 4.3 fusion.115
  1432.2 4.3 fusion.115
  1459.8 4.3 fusion.115
  1473.6 4.3 fusion.115
  1487.4 4.3 fusion.115
  1537.9 29.8 %fusion.32 = f32[512,36,128]{0,2,1:T(8,128)} fusion(bf16[128,36,512]{2,0,1:T(8,128)(2,1)} %all-gather.12.cloned.1.call-done, bf16[16,8,36,36,128]{4,1,0,3,2:T(8,128)(2,1)} %get-tuple-element.46), kind=kOutput, calls=%fused_computation.38 | convolution fusion | flops 21743271936 | bytes 56623104 | tf_op jit(solution)/shard_map/bmdc,bdk->kmc/dot_general | solution.py:63
  1569.3 5.4 fusion.57
  1574.8 88.0 %reduce-scatter.4.cloned.1.call-done = f32[128,36,128]{0,2,1:T(8,128)} async-done(((f32[512,36,128]{0,2,1:T(8,128)}), f32[128,36,128]{0,2,1:T(8,128)}) %reduce-scatter.4.cloned.1.call-update) | async-done | bytes 2359312 | tf_op jit(solution)/shard_map/reduce_scatter | solution.py:62
  1665.9 42.5 %all-reduce.14.cloned.1.call-done = bf16[128,512]{1,0:T(8,128)(2,1)} async-done(((bf16[128,512]{1,0:T(8,128)(2,1)}), bf16[128,512]{1,0:T(8,128)(2,1)}) %all-reduce.14.cloned.1.call-update) | async-done | bytes 131088 | tf_op jit(solution)/shard_map/psum | solution.py:93
  1708.4 5.1 multiply_bitcast_fusion
  (185 shorter events, 343.2 us)
Async XLA Ops:
  7.2 355.5 %copy-start = (bf16[1,512,128]{2,1,0:T(8,128)(2,1)S(1)}, bf16[1,512,128]{2,1,0:T(8,128)(2,1)}, u32[]{:S(2)}) copy-start(bf16[1,512,128]{2,1,0:T(8,128)(2,1)} %param.14) | copy-start | bytes 393220
  7.2 62.5 %all-gather.28.cloned.1.call-start = ((), (), s32[]{:S(2)}) async-start(), calls=%async_computation.19 | async-start | bytes 5898240 | tf_op jit(solution)/shard_map/all_gather | solution.py:54
  7.9 516.2 %reduce-scatter.6.cloned.1.call-start = ((), (), s32[]{:S(2)}) async-start(), calls=%async_computation.5 | async-start | bytes 11796480 | tf_op jit(solution)/shard_map/reduce_scatter | solution.py:76
  362.6 184.8 %reduce-scatter.8.cloned.1.call-start = ((), (), s32[]{:S(2)}) async-start(), calls=%async_computation.7 | async-start | bytes 327680 | tf_op jit(solution)/shard_map/reduce_scatter | solution.py:77
  370.0 268.8 %all-gather.14.cloned.1.call-start = ((), (), s32[]{:S(2)}) async-start(), calls=%async_computation.6 | async-start | bytes 5898240 | tf_op jit(solution)/shard_map/all_gather | solution.py:80
  527.0 243.7 %all-gather.16.cloned.1.call-start = ((), (), s32[]{:S(2)}) async-start(), calls=%async_computation.8 | async-start | bytes 5898240 | tf_op jit(solution)/shard_map/all_gather | solution.py:90
  684.1 132.4 %all-reduce.6.cloned.1.call-start = ((), (), s32[]{:S(2)}) async-start(), calls=%async_computation.9 | async-start | bytes 262144 | tf_op jit(solution)/shard_map/psum | solution.py:93
  776.2 135.2 %all-gather.18.cloned.1.call-start = ((), (), s32[]{:S(2)}) async-start(), calls=%async_computation.10 | async-start | bytes 5898240 | tf_op jit(solution)/shard_map/all_gather | solution.py:90
  822.1 135.9 %copy-start.3 = (f32[128,36,128]{2,0,1:T(8,128)S(1)}, f32[128,36,128]{2,0,1:T(8,128)}, u32[]{:S(2)}) copy-start(f32[128,36,128]{2,0,1:T(8,128)} %get-tuple-element.97) | copy-start | bytes 7077892
  822.1 135.8 %all-reduce.8.cloned.1.call-start = ((), (), s32[]{:S(2)}) async-start(), calls=%async_computation.11 | async-start | bytes 262144 | tf_op jit(solution)/shard_map/psum | solution.py:93
  917.6 135.2 %all-gather.20.cloned.1.call-start = ((), (), s32[]{:S(2)}) async-start(), calls=%async_computation.12 | async-start | bytes 5898240 | tf_op jit(solution)/shard_map/all_gather | solution.py:90
  963.5 135.8 %all-reduce.10.cloned.1.call-start = ((), (), s32[]{:S(2)}) async-start(), calls=%async_computation.13 | async-start | bytes 262144 | tf_op jit(solution)/shard_map/psum | solution.py:93
  1058.9 135.2 %all-gather.22.cloned.1.call-start = ((), (), s32[]{:S(2)}) async-start(), calls=%async_computation.14 | async-start | bytes 5898240 | tf_op jit(solution)/shard_map/all_gather | solution.py:90
  1104.9 146.3 %all-gather.26.cloned.1.call-start = ((), (), s32[]{:S(2)}) async-start(), calls=%async_computation.18 | async-start | bytes 5898240 | tf_op jit(solution)/shard_map/all_gather | solution.py:53
  1105.4 191.2 %all-reduce.12.cloned.1.call-start = ((), (), s32[]{:S(2)}) async-start(), calls=%async_computation.15 | async-start | bytes 262144 | tf_op jit(solution)/shard_map/psum | solution.py:93
  1105.5 94.2 %collective-permute-start = (bf16[128,36,128]{2,0,1:T(8,128)(2,1)}, bf16[128,36,128]{2,0,1:T(8,128)(2,1)}, u32[]{:S(2)}, u32[]{:S(2)}) collective-permute-start(bf16[128,36,128]{2,0,1:T(8,128)(2,1)} %bitcast.242), channel_id=1, source_target_pairs={{1,0},{0,1},{3,2},{2,3},{5,4},{4,5},{7,6},{6,7},{9,8},{8,9},{11,10... | collective-permute-start | bytes 3538952 | tf_op jit(solution)/shard_map/ppermute | solution.py:15
  1199.6 338.3 %all-gather.12.cloned.1.call-start = ((), (), s32[]{:S(2)}) async-start(), calls=%async_computation.3 | async-start | bytes 5898240 | tf_op jit(solution)/shard_map/all_gather | solution.py:61
  1200.2 367.8 %all-gather.24.cloned.1.call-start = ((), (), s32[]{:S(2)}) async-start(), calls=%async_computation.16 | async-start | bytes 5898240 | tf_op jit(solution)/shard_map/all_gather | solution.py:90
  1302.2 360.7 %reduce-scatter.4.cloned.1.call-start = ((), (), s32[]{:S(2)}) async-start(), calls=%async_computation.4 | async-start | bytes 11796480 | tf_op jit(solution)/shard_map/reduce_scatter | solution.py:62
  1567.7 1.7 copy-start.2
  1567.7 140.7 %all-reduce.14.cloned.1.call-start = ((), (), s32[]{:S(2)}) async-start(), calls=%async_computation.17 | async-start | bytes 262144 | tf_op jit(solution)/shard_map/psum | solution.py:93
  1662.8 50.7 %copy-start.1 = (bf16[1,512,128]{2,1,0:T(8,128)(2,1)S(1)}, bf16[1,512,128]{2,1,0:T(8,128)(2,1)}, u32[]{:S(2)}) copy-start(bf16[1,512,128]{2,1,0:T(8,128)(2,1)} %param.14) | copy-start | bytes 393220
Sparse Core Ops, SparseCore 0:
  9.9 59.7 all-gather.27
  362.8 161.2 reduce-scatter.5
  526.9 20.4 reduce-scatter.7
  549.5 89.1 all-gather.13
  684.2 86.4 all-gather.15
  776.3 40.1 all-reduce.5
  822.2 89.1 all-gather.17
  917.7 40.1 all-reduce.7
  963.6 89.1 all-gather.19
  1059.1 40.1 all-reduce.9
  1105.0 89.1 all-gather.21
  1195.8 55.2 all-gather.25
  1254.6 41.9 all-reduce.11
  1298.1 89.1 all-gather.11
  1389.3 87.3 all-gather.23
  1567.8 94.9 reduce-scatter.3
  1666.4 41.9 all-reduce.13
where the time goes:
time: 1730 us; the launch traced here: 1720 us
  waiting for transfers between devices  976 us (56%)
  matrix products  408 us (24%)
  local copies, waits for them, and re-layouts  252 us (15%)
  blocking collectives  61.2 us (4%)
    all_gather x5, waiting for transfers between devices, shards(): lax.all_gather(current.astype(jnp.bfloat16), 'dl', axis=2, tiled=True)  353 us
    psum x5, waiting for transfers between devices, shards(): lax.psum(jnp.einsum('bdx,bdy->xy', current, spread, precision=HIGHEST).as...  179 us
    reduce_scatter x1, waiting for transfers between devices, shards(): lax.psum_scatter(center_term, 'dl', scatter_dimension=0, tiled=True)  154 us
    dot_general x32, matrix products, layered(): jnp.einsum('bLUcrdp,LUsep->brsdec', ket_side, tensor, preferred_element_t...  138 us
    convert_element_type x32, local copies, waits for them, and re-layouts, layered(): both_sides.reshape(amount, leg_size * leg_size, leg_size * leg_size, colu...  98.5 us
    reduce_scatter x1, waiting for transfers between devices, shards(): lax.psum_scatter(jnp.einsum('bmdc,bdk->kmc', left_cut, bra_iso, preferred...  88 us
    dot_general x32, matrix products, layered(): jnp.einsum('blLuUc,lurdp->bLUcrdp', unfolded, tensor, preferred_element_t...  84.9 us
    all_gather x1, waiting for transfers between devices, shards(): lax.all_gather(center_part.astype(jnp.bfloat16), 'dl', axis=0, tiled=True)  68.2 us
  transfers between devices with their start and end apart: 18, of which 15 were waited for; matrix products, arithmetic and copies ran while one was open for 19% of the time, Pallas kernels for 0%

commit v1 on v0

--- a/solution.py
+++ b/solution.py
@@ -90,9 +90,12 @@
         spread = lax.all_gather(current.astype(jnp.bfloat16), "dl", axis=2, tiled=True).astype(
             current.dtype
         )
-        gram_rows = lax.psum(
-            jnp.einsum("bdx,bdy->xy", current, spread, precision=HIGHEST).astype(jnp.bfloat16),
-            "chi",
+        gram_rows = jnp.sum(
+            lax.all_gather(
+                jnp.einsum("bdx,bdy->xy", current, spread, precision=HIGHEST).astype(jnp.bfloat16),
+                "chi",
+            ),
+            axis=0,
         ).astype(jnp.float32)
         current = 1.5 * current - 0.5 * jnp.einsum(
             "bdy,xy->bdx", spread, gram_rows, precision=HIGHEST

time: 1730 us -> 1540 us (0.89)
  waiting for transfers between devices: 976 us -> 718 us
  blocking collectives: 61.2 us -> 121 us
    psum x5 -> x0, waiting for transfers between devices: 179 us -> none  [shards(): lax.psum(jnp.einsum('bdx,bdy->xy', current, spread, precision=HIGHEST).as...]
    all_gather x0 -> x5, blocking collectives: none -> 59.8 us  [shards(): lax.all_gather(jnp.einsum('bdx,bdy->xy', current, spread, precision=HIGHE...]
    all_gather x5, waiting for transfers between devices: 353 us -> 312 us  [shards(): lax.all_gather(current.astype(jnp.bfloat16), 'dl', axis=2, tiled=True)]
    all_gather x1, waiting for transfers between devices: 50.5 us -> 29 us  [shards(): lax.all_gather(left_iso, 'chi', axis=0, tiled=True)]
    reduce_scatter x1, waiting for transfers between devices: 88 us -> 69.6 us  [shards(): lax.psum_scatter(jnp.einsum('bmdc,bdk->kmc', left_cut, bra_iso, preferred...]
  transfers between devices with their start and end apart: 18 -> 13, of which waited for: 15 -> 11; matrix products, arithmetic and copies ran while one was open for 19% -> 22% of each run, Pallas kernels for 0% -> 0%
where the time goes in v1:
time: 1540 us; the launch traced here: 1530 us
  waiting for transfers between devices  718 us (47%)
  matrix products  404 us (26%)
  local copies, waits for them, and re-layouts  252 us (16%)
  blocking collectives  121 us (8%)
  between operations  15.4 us (1%)
    all_gather x5, waiting for transfers between devices, shards(): lax.all_gather(current.astype(jnp.bfloat16), 'dl', axis=2, tiled=True)  312 us
    reduce_scatter x1, waiting for transfers between devices, shards(): lax.psum_scatter(center_term, 'dl', scatter_dimension=0, tiled=True)  154 us
    dot_general x32, matrix products, layered(): jnp.einsum('bLUcrdp,LUsep->brsdec', ket_side, tensor, preferred_element_t...  138 us
    convert_element_type x32, local copies, waits for them, and re-layouts, layered(): both_sides.reshape(amount, leg_size * leg_size, leg_size * leg_size, colu...  98.5 us
    dot_general x32, matrix products, layered(): jnp.einsum('blLuUc,lurdp->bLUcrdp', unfolded, tensor, preferred_element_t...  85 us
    reduce_scatter x1, waiting for transfers between devices, shards(): lax.psum_scatter(jnp.einsum('bmdc,bdk->kmc', left_cut, bra_iso, preferred...  69.6 us
    all_gather x1, waiting for transfers between devices, shards(): lax.all_gather(center_part.astype(jnp.bfloat16), 'dl', axis=0, tiled=True)  68.1 us
    dynamic_slice x32, local copies, waits for them, and re-layouts, through_site(): finished = lax.map(partial(layered, tensor=tensor), blocks)  61.6 us
  transfers between devices with their start and end apart: 13, of which 11 were waited for; matrix products, arithmetic and copies ran while one was open for 22% of the time, Pallas kernels for 0%

profile of v1, /device:TPU:0, one launch (start us, length us, event | category | flops | bytes accessed | tf_op | source)
XLA Modules:
  0.0 1527.5 jit_solution(13196005107903824257)
XLA Ops:
  9.4 60.3 %all-gather.33.cloned.1.call-done = bf16[1,512,36,128]{3,1,2,0:T(8,128)(2,1)} async-done(((bf16[1,128,36,128]{3,1,2,0:T(8,128)(2,1)}), bf16[1,512,36,128]{3,1,2,0:T(8,128)(2,1)}) %all-gather.33.cloned.1.call-update) | async-done | bytes 4718608 | tf_op jit(solution)/shard_map/all_gather | solution.py:54
  69.7 29.5 %convert_bitcast_fusion = bf16[16,8,36,36,128]{4,1,0,3,2:T(8,128)(2,1)} fusion(bf16[1,512,128,36]{2,1,3,0:T(8,128)(2,1)} %param.10, bf16[1,512,36,128]{3,1,2,0:T(8,128)(2,1)} %all-gather.33.cloned.1.call-done), kind=kOutput, calls=%fused_computation.26 | convolution fusion | flops 21764505600 | bytes 51904512 | tf_op jit(solution)/shard_map/abm,asc->bmsc/dot_general | solution.py:58
  99.2 14.1 broadcast.9.clone2.1
  113.3 220.7 %while.21 = (s32[]{:T(128)}, bf16[16,8,36,36,128]{4,1,0,3,2:T(8,128)(2,1)}, bf16[16,8,36,36,128]{4,1,0,3,2:T(8,128)(2,1)}, bf16[6,6,6,6,2]{1,3,4,0,2:T(8,128)(2,1)S(1)}, s32[]{:T(128)}) while((s32[]{:T(128)}, bf16[16,8,36,36,128]{4,1,0,3,2:T(8,128)(2,1)}, bf16[16,8,36,36,128]{4,1,0,3,2:T(8,128)(2,1)}, bf16[6,6,6,6,2]{1,3,4,0,2:T(8,128)(2,1)S(1)}, ...), condition=%wide.region_4.5_spmd, body=%wide.region_3.4_spmd.sunk | while | flops 386187264 | bytes 31861440 | solution.py:38
  117.9 4.3 fusion.122
  131.7 4.3 fusion.122
  159.3 4.3 fusion.122
  173.1 4.3 fusion.122
  186.9 4.3 fusion.122
  200.7 4.3 fusion.122
  214.4 4.3 fusion.122
  228.2 4.3 fusion.122
  242.0 4.3 fusion.122
  269.7 4.3 fusion.122
  283.4 4.3 fusion.122
  297.2 4.3 fusion.122
  311.0 4.3 fusion.122
  334.0 28.7 %fusion.37 = f32[512,128,36]{0,1,2:T(8,128)} fusion(bf16[1,128,36,512]{3,1,2,0:T(8,128)(2,1)} %param.13, bf16[16,8,36,36,128]{4,1,0,3,2:T(8,128)(2,1)} %get-tuple-element.47), kind=kOutput, calls=%fused_computation.39 | convolution fusion | flops 21743271936 | bytes 56623104 | tf_op jit(solution)/shard_map/bmda,amc->cbd/dot_general | solution.py:68
  362.8 7.2 fusion.51
  370.1 154.1 %reduce-scatter.6.cloned.1.call-done = f32[128,128,36]{0,1,2:T(8,128)} async-done(((f32[512,128,36]{0,1,2:T(8,128)}), f32[128,128,36]{0,1,2:T(8,128)}) %reduce-scatter.6.cloned.1.call-update) | async-done | bytes 2359312 | tf_op jit(solution)/shard_map/reduce_scatter | solution.py:76
  527.1 20.4 %reduce-scatter.8.cloned.1.call-done = f32[128,128]{0,1:T(8,128)} async-done(((f32[512,128]{0,1:T(8,128)}), f32[128,128]{0,1:T(8,128)}) %reduce-scatter.8.cloned.1.call-update) | async-done | bytes 65552 | tf_op jit(solution)/shard_map/reduce_scatter | solution.py:77
  548.4 12.3 all_gather.67
  560.7 10.0 all_gather.68
  570.7 68.1 %all-gather.19.cloned.1.call-done = bf16[512,128,36]{0,1,2:T(8,128)(2,1)} async-done(((bf16[128,128,36]{0,1,2:T(8,128)(2,1)}), bf16[512,128,36]{0,1,2:T(8,128)(2,1)}) %all-gather.19.cloned.1.call-update) | async-done | bytes 4718608 | tf_op jit(solution)/shard_map/all_gather | solution.py:80
  638.9 4.3 multiply_reduce_fusion
  643.2 38.9 %psum.7 = f32[]{:T(128)} all-reduce(f32[]{:T(128)} %get-tuple-element.94), channel_id=1, replica_groups=mesh['chi'=4,'dl'=4,'cell'=2] {'chi','dl'}, use_global_device_ids=true, to_apply=%region_8.9 | all-reduce | flops 1 | bytes 8 | tf_op jit(solution)/shard_map/psum | solution.py:87
  684.2 86.6 %all-gather.21.cloned.1.call-done = bf16[128,36,512]{2,0,1:T(8,128)(2,1)} async-done(((bf16[128,36,128]{2,0,1:T(8,128)(2,1)}), bf16[128,36,512]{2,0,1:T(8,128)(2,1)}) %all-gather.21.cloned.1.call-update) | async-done | bytes 4718608 | tf_op jit(solution)/shard_map/all_gather | solution.py:90
  770.8 4.8 fusion.58
  775.6 10.0 all-gather.2
  785.7 5.5 fusion.74
  792.0 10.0 all-gather.25.cloned.1.call-start
  802.0 75.8 %all-gather.23.cloned.1.call-done = bf16[128,36,512]{2,0,1:T(8,128)(2,1)} async-done(((bf16[128,36,128]{2,0,1:T(8,128)(2,1)}), bf16[128,36,512]{2,0,1:T(8,128)(2,1)}) %all-gather.23.cloned.1.call-update) | async-done | bytes 4718608 | tf_op jit(solution)/shard_map/all_gather | solution.py:90
  877.8 5.5 fusion.54
  883.3 15.0 all-gather.3
  898.4 5.5 fusion.75
  907.3 29.0 %all-gather.31.cloned.1.call-done = bf16[1,512,36,128]{3,1,2,0:T(8,128)(2,1)} async-done(((bf16[1,128,36,128]{3,1,2,0:T(8,128)(2,1)}), bf16[1,512,36,128]{3,1,2,0:T(8,128)(2,1)}) %all-gather.31.cloned.1.call-update) | async-done | bytes 4718608 | tf_op jit(solution)/shard_map/all_gather | solution.py:53
  936.4 29.5 %convert_bitcast_fusion.1 = bf16[16,8,36,36,128]{4,1,0,3,2:T(8,128)(2,1)} fusion(bf16[1,512,128,36]{2,1,3,0:T(8,128)(2,1)} %param.10, bf16[1,512,36,128]{3,1,2,0:T(8,128)(2,1)} %all-gather.31.cloned.1.call-done), kind=kOutput, calls=%fused_computation.27 | convolution fusion | flops 21764505600 | bytes 51904512 | tf_op jit(solution)/shard_map/abm,asc->bmsc/dot_general | solution.py:56
  965.9 61.8 %all-gather.25.cloned.1.call-done = bf16[128,36,512]{2,0,1:T(8,128)(2,1)} async-done(((bf16[128,36,128]{2,0,1:T(8,128)(2,1)}), bf16[128,36,512]{2,0,1:T(8,128)(2,1)}) %all-gather.25.cloned.1.call-update) | async-done | bytes 4718608 | tf_op jit(solution)/shard_map/all_gather | solution.py:90
  1027.7 4.8 fusion.55
  1032.5 10.0 all-gather.4
  1042.6 5.5 fusion.76
  1048.4 14.1 broadcast.9.clone2
  1062.6 220.8 %while.20 = (s32[]{:T(128)}, bf16[16,8,36,36,128]{4,1,0,3,2:T(8,128)(2,1)}, bf16[16,8,36,36,128]{4,1,0,3,2:T(8,128)(2,1)}, bf16[6,6,6,6,2]{1,3,4,0,2:T(8,128)(2,1)S(1)}, s32[]{:T(128)}) while((s32[]{:T(128)}, bf16[16,8,36,36,128]{4,1,0,3,2:T(8,128)(2,1)}, bf16[16,8,36,36,128]{4,1,0,3,2:T(8,128)(2,1)}, bf16[6,6,6,6,2]{1,3,4,0,2:T(8,128)(2,1)S(1)}, ...), condition=%wide.region_1.2_spmd, body=%wide.region_0.1_spmd.sunk | while | flops 386187264 | bytes 31861440 | solution.py:38
  1067.2 4.3 fusion.115
  1108.6 4.3 fusion.115
  1122.3 4.3 fusion.115
  1136.2 4.3 fusion.115
  1163.8 4.3 fusion.115
  1177.6 4.3 fusion.115
  1191.4 4.3 fusion.115
  1219.1 4.3 fusion.115
  1232.8 4.3 fusion.115
  1246.6 4.3 fusion.115
  1260.4 4.3 fusion.115
  1274.2 4.3 fusion.115
  1283.4 29.7 %fusion.32 = f32[512,36,128]{0,2,1:T(8,128)} fusion(bf16[128,36,512]{2,0,1:T(8,128)(2,1)} %all-gather.17.cloned.1.call-done, bf16[16,8,36,36,128]{4,1,0,3,2:T(8,128)(2,1)} %get-tuple-element.46), kind=kOutput, calls=%fused_computation.38 | convolution fusion | flops 21743271936 | bytes 56623104 | tf_op jit(solution)/shard_map/bmdc,bdk->kmc/dot_general | solution.py:63
  1314.7 4.8 fusion.56
  1319.5 14.8 all-gather.5
  1334.4 5.5 fusion.77
  1340.0 69.6 %reduce-scatter.4.cloned.1.call-done = f32[128,36,128]{0,2,1:T(8,128)} async-done(((f32[512,36,128]{0,2,1:T(8,128)}), f32[128,36,128]{0,2,1:T(8,128)}) %reduce-scatter.4.cloned.1.call-update) | async-done | bytes 2359312 | tf_op jit(solution)/shard_map/reduce_scatter | solution.py:62
  1412.6 87.6 %all-gather.29.cloned.1.call-done = bf16[128,36,512]{2,0,1:T(8,128)(2,1)} async-done(((bf16[128,36,128]{2,0,1:T(8,128)(2,1)}), bf16[128,36,512]{2,0,1:T(8,128)(2,1)}) %all-gather.29.cloned.1.call-update) | async-done | bytes 4718608 | tf_op jit(solution)/shard_map/all_gather | solution.py:90
  1500.2 4.8 fusion.57
  1505.0 10.0 all-gather.6
  1515.1 5.1 multiply_bitcast_fusion
  (180 shorter events, 349.9 us)
Async XLA Ops:
  7.2 355.6 %copy-start = (bf16[1,512,128]{2,1,0:T(8,128)(2,1)S(1)}, bf16[1,512,128]{2,1,0:T(8,128)(2,1)}, u32[]{:S(2)}) copy-start(bf16[1,512,128]{2,1,0:T(8,128)(2,1)} %param.14) | copy-start | bytes 393220
  7.2 62.5 %all-gather.33.cloned.1.call-start = ((), (), s32[]{:S(2)}) async-start(), calls=%async_computation.14 | async-start | bytes 5898240 | tf_op jit(solution)/shard_map/all_gather | solution.py:54
  7.9 516.3 %reduce-scatter.6.cloned.1.call-start = ((), (), s32[]{:S(2)}) async-start(), calls=%async_computation.5 | async-start | bytes 11796480 | tf_op jit(solution)/shard_map/reduce_scatter | solution.py:76
  362.7 184.8 %reduce-scatter.8.cloned.1.call-start = ((), (), s32[]{:S(2)}) async-start(), calls=%async_computation.7 | async-start | bytes 327680 | tf_op jit(solution)/shard_map/reduce_scatter | solution.py:77
  370.1 268.8 %all-gather.19.cloned.1.call-start = ((), (), s32[]{:S(2)}) async-start(), calls=%async_computation.6 | async-start | bytes 5898240 | tf_op jit(solution)/shard_map/all_gather | solution.py:80
  527.1 243.7 %all-gather.21.cloned.1.call-start = ((), (), s32[]{:S(2)}) async-start(), calls=%async_computation.8 | async-start | bytes 5898240 | tf_op jit(solution)/shard_map/all_gather | solution.py:90
  684.2 193.6 %all-gather.23.cloned.1.call-start = ((), (), s32[]{:S(2)}) async-start(), calls=%async_computation.9 | async-start | bytes 5898240 | tf_op jit(solution)/shard_map/all_gather | solution.py:90
  791.2 145.1 %all-gather.31.cloned.1.call-start = ((), (), s32[]{:S(2)}) async-start(), calls=%async_computation.13 | async-start | bytes 5898240 | tf_op jit(solution)/shard_map/all_gather | solution.py:53
  792.0 235.8 %all-gather.25.cloned.1.call-start = ((), (), s32[]{:S(2)}) async-start(), calls=%async_computation.10 | async-start | bytes 5898240 | tf_op jit(solution)/shard_map/all_gather | solution.py:90
  904.0 379.4 %all-gather.17.cloned.1.call-start = ((), (), s32[]{:S(2)}) async-start(), calls=%async_computation.3 | async-start | bytes 5898240 | tf_op jit(solution)/shard_map/all_gather | solution.py:61
  904.0 3.3 collective-permute-start
  907.3 406.1 %all-gather.27.cloned.1.call-start = ((), (), s32[]{:S(2)}) async-start(), calls=%async_computation.11 | async-start | bytes 5898240 | tf_op jit(solution)/shard_map/all_gather | solution.py:90
  1048.2 361.3 %reduce-scatter.4.cloned.1.call-start = ((), (), s32[]{:S(2)}) async-start(), calls=%async_computation.4 | async-start | bytes 11796480 | tf_op jit(solution)/shard_map/reduce_scatter | solution.py:62
  1313.1 1.7 copy-start.2
  1313.1 187.1 %all-gather.29.cloned.1.call-start = ((), (), s32[]{:S(2)}) async-start(), calls=%async_computation.12 | async-start | bytes 5898240 | tf_op jit(solution)/shard_map/all_gather | solution.py:90
  1339.9 160.2 %copy-start.3 = (f32[128,36,128]{2,0,1:T(8,128)S(1)}, f32[128,36,128]{2,0,1:T(8,128)}, u32[]{:S(2)}) copy-start(f32[128,36,128]{2,0,1:T(8,128)} %get-tuple-element.103) | copy-start | bytes 7077892
  1515.0 5.2 copy-start.1
Sparse Core Ops, SparseCore 0:
  9.9 59.7 all-gather.32
  362.8 161.2 reduce-scatter.5
  527.0 20.4 reduce-scatter.7
  549.6 89.1 all-gather.18
  684.3 86.4 all-gather.20
  791.3 86.3 all-gather.22
  879.8 56.5 all-gather.30
  938.6 89.1 all-gather.24
  1029.4 87.3 all-gather.16
  1118.8 87.3 all-gather.26
  1313.2 96.2 reduce-scatter.3
  1411.0 89.1 all-gather.28
